TPU v7x, 512 devices: a whole 4x4x16 slice. The times are simulated.
512 devices in a mesh: rows: 64 (over z, y), cols: 8 (over x, core).
Axes of the slice: x: 4, y: 4, z: 16, core: 2. Of those that a mesh axis runs over, the one named last changes fastest.
Arguments:
- sens_base: bfloat16 [524288, 1024], P('rows', 'cols'), may hold values from -0.14157282 to 0.14157282
- design_field: float32 [512, 1024], P('rows'), may hold values from -3 to 3
- gradient: bfloat16 [512, 1024], P('rows'), may hold values from -6 to 6
- tile_index: int32 [1024], P('cols'), may hold values from 0 to 31
- type_codes: int32 [1024], P('cols'), may hold values from 0 to 2
Outputs:
- r_panels: float32 [512, 1024], P(None, 'cols')
- multipliers: float32 [512], replicated
Inputs may be any that keep to these rules, and one draw needn't show every extreme that they name: `tile_index`: each constraint names one support tile.
All inputs are finite; a program needn't handle non-finite values.
Results may differ from a plain program's by a relative error of at most 0.0003.
The roundings to bfloat16 on the way count: a program that leaves them out, or rounds other values in their place, can miss the bound.
Values may be sent and summed in bfloat16 or wider, within the bound.
A program may use at most 64 MiB of HBM per device.

v0:
```python
import math
import jax
import jax.numpy as jnp
from jax import lax
from jax.sharding import PartitionSpec as P

TILE = 128
PW = 256


def padded_2(cells, sides, width):
    for axis, dim in sides:
        count = lax.axis_size(axis)
        ends = count - 1
        head = lax.slice_in_dim(cells, 0, width, axis=dim)
        tail = lax.slice_in_dim(cells, cells.shape[dim] - width, cells.shape[dim], axis=dim)
        cells = jnp.concatenate(
            [
                lax.ppermute(tail, axis, [(i, (i + 1) % count) for i in range(ends)]),
                cells,
                lax.ppermute(head, axis, [((i + 1) % count, i) for i in range(ends)]),
            ],
            axis=dim,
        )
    return cells


def assemble(base_cols, tile_cols, type_cols, stencils, cell_tile):
    kinds_all = jnp.arange(3, dtype=jnp.int32)
    chooser = (type_cols[None, :] == kinds_all[:, None]).astype(jnp.float32)
    picked = lax.dot_general(
        stencils,
        chooser,
        (((0,), (0,)), ((), ())),
        precision=lax.Precision.HIGHEST,
        preferred_element_type=jnp.float32,
    )
    inside = cell_tile[:, None] == tile_cols[None, :]
    total = base_cols.astype(jnp.float32) + jnp.where(inside, picked / TILE, 0.0)
    return total.astype(jnp.bfloat16)


def matmul(left, right):
    return jnp.dot(left, right, precision=lax.Precision.HIGHEST, preferred_element_type=jnp.float32)


def small_factor(matrix):
    order = matrix.shape[0]
    positions = jnp.arange(order, dtype=jnp.int32)

    def column_step(index_col, carry):
        working, lower = carry
        column = lax.dynamic_slice_in_dim(working, index_col, 1, 1)[:, 0]
        pivot = jnp.sqrt(lax.dynamic_slice_in_dim(column, index_col, 1, 0)[0])
        column = jnp.where(positions >= index_col, column / pivot, 0.0)
        lower = jnp.where(positions[None, :] == index_col, column[:, None], lower)
        working = working - column[:, None] * column[None, :]
        return (working, lower)

    return lax.fori_loop(0, order, column_step, (matrix, jnp.zeros_like(matrix)))[1]


def small_inverse(lower):
    order = lower.shape[0]
    positions = jnp.arange(order, dtype=jnp.int32)
    right = jnp.eye(order, dtype=jnp.float32)

    def row_step(index_row, carry):
        rest, solved = carry
        column = lax.dynamic_slice_in_dim(lower, index_row, 1, 1)[:, 0]
        pivot = lax.dynamic_slice_in_dim(column, index_row, 1, 0)[0]
        value = lax.dynamic_slice_in_dim(rest, index_row, 1, 0) / pivot
        solved = jnp.where(positions[:, None] == index_row, value, solved)
        below = jnp.where(positions > index_row, column, 0.0)
        rest = rest - below[:, None] * value
        return (rest, solved)

    return lax.fori_loop(0, order, row_step, (right, jnp.zeros_like(right)))[1]


def factor_lower(matrix):
    order = matrix.shape[0]
    width = math.gcd(order, 32)
    working = matrix
    lower = jnp.zeros_like(matrix)
    inverses = []
    for block_num in range(order // width):
        start = block_num * width
        diag_lower = small_factor(working[:width, :width])
        diag_inverse = small_inverse(diag_lower)
        inverses.append(diag_inverse)
        lower = lower.at[start : start + width, start : start + width].set(diag_lower)
        if start + width < order:
            panel = matmul(working[width:, :width], diag_inverse.T)
            lower = lower.at[start + width :, start : start + width].set(panel)
            working = working[width:, width:] - matmul(panel, panel.T)
    return (lower, inverses)


def solve_forward(lower, inverses, right):
    width = inverses[0].shape[0]
    solved = []
    for block_num in range(len(inverses)):
        start = block_num * width
        rest = right[start : start + width]
        if block_num > 0:
            rest = rest - matmul(
                lower[start : start + width, :start], jnp.concatenate(solved, axis=0)
            )
        solved.append(matmul(inverses[block_num], rest))
    return jnp.concatenate(solved, axis=0)


def solve_backward(lower, inverses, right):
    width = inverses[0].shape[0]
    order = lower.shape[0]
    solved = []
    for block_num in reversed(range(len(inverses))):
        start = block_num * width
        rest = right[start : start + width]
        if start + width < order:
            rest = rest - matmul(
                lower[start + width :, start : start + width].T, jnp.concatenate(solved, axis=0)
            )
        solved.insert(0, matmul(inverses[block_num].T, rest))
    return jnp.concatenate(solved, axis=0)


def shards(sens_base, design_field, gradient, tile_index, type_codes):
    rows_here = design_field.shape[0]
    grid_width = design_field.shape[1]
    cols_here = sens_base.shape[1]
    factored = 2 * PW
    padded = padded_2(design_field, (("rows", 0),), 1)
    padded = jnp.pad(padded, ((0, 0), (1, 1)))
    north_cells = padded[:-2, 1:-1]
    south_cells = padded[2:, 1:-1]
    west_cells = padded[1:-1, :-2]
    east_cells = padded[1:-1, 2:]
    laplace = 4.0 * design_field - (north_cells + south_cells + west_cells + east_cells)
    slope_x = 0.5 * (east_cells - west_cells)
    slope_y = 0.5 * (south_cells - north_cells)
    stencils = jnp.stack([laplace, slope_x, slope_y]).reshape(3, -1)
    row_glob = lax.axis_index("rows") * rows_here + jnp.arange(rows_here, dtype=jnp.int32)
    col_ids = jnp.arange(grid_width, dtype=jnp.int32) // TILE
    cell_tile = ((row_glob // TILE)[:, None] * (grid_width // TILE) + col_ids[None, :]).reshape(-1)
    local_jac = assemble(sens_base, tile_index, type_codes, stencils, cell_tile)
    grad_flat = gradient.reshape(-1)
    row_major = lax.all_to_all(local_jac, "cols", split_axis=0, concat_axis=1, tiled=True)
    row_piece = row_major.shape[0]
    grad_part = lax.dynamic_slice_in_dim(
        grad_flat, lax.axis_index("cols") * row_piece, row_piece, 0
    )
    leading = row_major[:, :factored]
    gram_block = lax.dot_general(
        leading, row_major, (((0,), (0,)), ((), ())), preferred_element_type=jnp.float32
    )
    projected = jnp.dot(grad_part, leading, preferred_element_type=jnp.float32)
    gram_block, projected = lax.psum((gram_block, projected), ("rows", "cols"))
    gram_head = gram_block[:, :factored]
    gram_own = lax.dynamic_slice_in_dim(
        gram_block, lax.axis_index("cols") * cols_here, cols_here, 1
    )
    lower_chol, inverses = factor_lower(gram_head)
    r_panels = solve_forward(lower_chol, inverses, gram_own)
    half_solved = solve_forward(lower_chol, inverses, projected[:, None])
    multipliers = solve_backward(lower_chol, inverses, half_solved)[:, 0]
    return (r_panels, multipliers)


def solution(mesh):
    placed = (P("rows", "cols"), P("rows", None), P("rows", None), P("cols"), P("cols"))
    return jax.shard_map(
        shards, mesh=mesh, in_specs=placed, out_specs=(P(None, "cols"), P()), check_vma=False
    )
```

profile of v0, /device:TPU:1, one launch (start us, length us, event | category | flops | bytes accessed | tf_op | source)
XLA Modules:
  0.0 2140.8 jit_solution(14819654451309352459)
XLA Ops:
  8.1 4.0 collective-permute-start
  13.5 2.9 collective-permute-done.1
  18.4 6.7 fusion.98
  25.0 2.9 copy.37
  27.9 34.2 %all_to_all.19 = bf16[8,1024,128]{1,2,0:T(8,128)(2,1)S(1)} all-to-all(bf16[8,1024,128]{1,2,0:T(8,128)(2,1)S(1)} %copy.37), channel_id=1, replica_groups=mesh['rows'=64,'cols'=8] {'cols'}, dimensions={0} | all-to-all | bytes 4194304 | tf_op jit(solution)/shard_map/all_to_all | solution.py:149
  63.4 2.6 fusion.161
  68.0 110.2 %psum.15 = f32[512]{0:T(512)S(1)} all-reduce(f32[512]{0:T(512)S(1)} %bitcast.1236), channel_id=1, replica_groups=mesh['rows'=64,'cols'=8] {'rows','cols'}, use_global_device_ids=true, to_apply=%region_65.66 | all-reduce | flops 512 | bytes 4096 | tf_op jit(solution)/shard_map/psum | solution.py:159
  178.3 367.6 %all-reduce.4.cloned.1.call-done = f32[512,1024]{1,0:T(8,128)} async-done(((f32[512,1024]{1,0:T(8,128)}), f32[512,1024]{1,0:T(8,128)}) %all-reduce.4.cloned.1.call-update) | async-done | bytes 2097168 | tf_op jit(solution)/shard_map/psum | solution.py:159
  546.7 45.5 %while.671 = (s32[]{:T(128)}, f32[32,32]{0,1:T(8,128)S(1)}, f32[32,32]{0,1:T(8,128)S(1)}, s32[]{:T(128)}, s32[]{:T(128)}, /*index=5*/s32[]{:T(128)}) while((s32[]{:T(128)}, f32[32,32]{0,1:T(8,128)S(1)}, f32[32,32]{0,1:T(8,128)S(1)}, s32[]{:T(128)}, s32[]{:T(128)}, /*index=5*/s32[]{:T(128)}) %tuple.1741), condition=%wide.region_2.3_spmd.clone.clone, body=%wide.region_1.2_spmd.clone.clone.sunk | while | flops 4292 | bytes 19003 | solution.py:60
  592.2 43.6 %while.672 = (s32[]{:T(128)}, f32[32,32]{1,0:T(8,128)S(1)}, f32[32,32]{1,0:T(8,128)S(1)}, f32[32,32]{0,1:T(8,128)S(1)}, s32[]{:T(128)}, /*index=5*/s32[]{:T(128)}, s32[]{:T(128)}) while((s32[]{:T(128)}, f32[32,32]{1,0:T(8,128)S(1)}, f32[32,32]{1,0:T(8,128)S(1)}, f32[32,32]{0,1:T(8,128)S(1)}, s32[]{:T(128)}, ...), condition=%wide.region_4.5_spmd.clone.clone, body=%wide.region_3.4_spmd.clone.clone.sunk | while | flops 4228 | bytes 18367 | solution.py:78
  637.2 2.3 convolution_subtract_fusion
  639.5 45.0 %while.673 = (s32[]{:T(128)}, f32[32,32]{0,1:T(8,128)S(1)}, f32[32,32]{0,1:T(8,128)S(1)}, s32[]{:T(128)}, s32[]{:T(128)}, /*index=5*/s32[]{:T(128)}) while((s32[]{:T(128)}, f32[32,32]{0,1:T(8,128)S(1)}, f32[32,32]{0,1:T(8,128)S(1)}, s32[]{:T(128)}, s32[]{:T(128)}, /*index=5*/s32[]{:T(128)}) %tuple.1747), condition=%wide.region_6.7_spmd.clone.clone, body=%wide.region_5.6_spmd.clone.clone.sunk | while | flops 4292 | bytes 19003 | solution.py:60
  684.6 43.6 %while.674 = (s32[]{:T(128)}, f32[32,32]{1,0:T(8,128)S(1)}, f32[32,32]{1,0:T(8,128)S(1)}, f32[32,32]{0,1:T(8,128)S(1)}, s32[]{:T(128)}, /*index=5*/s32[]{:T(128)}, s32[]{:T(128)}) while((s32[]{:T(128)}, f32[32,32]{1,0:T(8,128)S(1)}, f32[32,32]{1,0:T(8,128)S(1)}, f32[32,32]{0,1:T(8,128)S(1)}, s32[]{:T(128)}, ...), condition=%wide.region_8.9_spmd.clone.clone, body=%wide.region_7.8_spmd.clone.clone.sunk | while | flops 4228 | bytes 18367 | solution.py:78
  729.6 45.0 %while.675 = (s32[]{:T(128)}, f32[32,32]{0,1:T(8,128)S(1)}, f32[32,32]{0,1:T(8,128)S(1)}, s32[]{:T(128)}, s32[]{:T(128)}, /*index=5*/s32[]{:T(128)}) while((s32[]{:T(128)}, f32[32,32]{0,1:T(8,128)S(1)}, f32[32,32]{0,1:T(8,128)S(1)}, s32[]{:T(128)}, s32[]{:T(128)}, /*index=5*/s32[]{:T(128)}) %tuple.1753), condition=%wide.region_10.11_spmd.clone.clone, body=%wide.region_9.10_spmd.clone.clone.sunk | while | flops 4292 | bytes 19003 | solution.py:60
  774.6 43.6 %while.676 = (s32[]{:T(128)}, f32[32,32]{1,0:T(8,128)S(1)}, f32[32,32]{1,0:T(8,128)S(1)}, f32[32,32]{0,1:T(8,128)S(1)}, s32[]{:T(128)}, /*index=5*/s32[]{:T(128)}, s32[]{:T(128)}) while((s32[]{:T(128)}, f32[32,32]{1,0:T(8,128)S(1)}, f32[32,32]{1,0:T(8,128)S(1)}, f32[32,32]{0,1:T(8,128)S(1)}, s32[]{:T(128)}, ...), condition=%wide.region_12.13_spmd.clone.clone, body=%wide.region_11.12_spmd.clone.clone.sunk | while | flops 4228 | bytes 18367 | solution.py:78
  819.6 86.6 %while.677 = (s32[]{:T(128)}, f32[32,32]{0,1:T(8,128)S(1)}, f32[32,32]{0,1:T(8,128)}, s32[]{:T(128)}, s32[]{:T(128)}, /*index=5*/s32[]{:T(128)}) while((s32[]{:T(128)}, f32[32,32]{0,1:T(8,128)S(1)}, f32[32,32]{0,1:T(8,128)}, s32[]{:T(128)}, s32[]{:T(128)}, /*index=5*/s32[]{:T(128)}) %tuple.1759), condition=%wide.region_14.15_spmd.clone.clone, body=%wide.region_13.14_spmd.clone.clone.sunk | while | flops 4292 | bytes 19003 | solution.py:60
  825.7 1.4 select_select_fusion.70
  906.4 1.4 scatter.101
  907.8 2.1 scatter.104
  909.9 1.4 scatter.105
  911.3 2.1 scatter.106
  913.4 1.4 scatter.109
  914.8 2.1 scatter.110
  917.0 86.4 %while.678 = (s32[]{:T(128)}, f32[32,32]{1,0:T(8,128)S(1)}, f32[32,32]{1,0:T(8,128)S(1)}, f32[32,32]{0,1:T(8,128)}, s32[]{:T(128)}, /*index=5*/s32[]{:T(128)}, s32[]{:T(128)}) while((s32[]{:T(128)}, f32[32,32]{1,0:T(8,128)S(1)}, f32[32,32]{1,0:T(8,128)S(1)}, f32[32,32]{0,1:T(8,128)}, s32[]{:T(128)}, ...), condition=%wide.region_16.17_spmd.clone.clone, body=%wide.region_15.16_spmd.clone.clone.sunk | while | flops 4228 | bytes 18751 | solution.py:78
  1004.5 45.0 %while.679 = (s32[]{:T(128)}, f32[32,32]{0,1:T(8,128)S(1)}, f32[32,32]{0,1:T(8,128)S(1)}, s32[]{:T(128)}, s32[]{:T(128)}, /*index=5*/s32[]{:T(128)}) while((s32[]{:T(128)}, f32[32,32]{0,1:T(8,128)S(1)}, f32[32,32]{0,1:T(8,128)S(1)}, s32[]{:T(128)}, s32[]{:T(128)}, /*index=5*/s32[]{:T(128)}) %tuple.1856), condition=%wide.region_18.19_spmd.clone.clone, body=%wide.region_17.18_spmd.clone.clone.sunk | while | flops 4292 | bytes 19003 | solution.py:60
  1049.5 43.6 %while.680 = (s32[]{:T(128)}, f32[32,32]{1,0:T(8,128)S(1)}, f32[32,32]{1,0:T(8,128)S(1)}, f32[32,32]{0,1:T(8,128)S(1)}, s32[]{:T(128)}, /*index=5*/s32[]{:T(128)}, s32[]{:T(128)}) while((s32[]{:T(128)}, f32[32,32]{1,0:T(8,128)S(1)}, f32[32,32]{1,0:T(8,128)S(1)}, f32[32,32]{0,1:T(8,128)S(1)}, s32[]{:T(128)}, ...), condition=%wide.region_20.21_spmd.clone.clone, body=%wide.region_19.20_spmd.clone.clone.sunk | while | flops 4228 | bytes 18367 | solution.py:78
  1094.1 45.0 %while.681 = (s32[]{:T(128)}, f32[32,32]{0,1:T(8,128)S(1)}, f32[32,32]{0,1:T(8,128)S(1)}, s32[]{:T(128)}, s32[]{:T(128)}, /*index=5*/s32[]{:T(128)}) while((s32[]{:T(128)}, f32[32,32]{0,1:T(8,128)S(1)}, f32[32,32]{0,1:T(8,128)S(1)}, s32[]{:T(128)}, s32[]{:T(128)}, /*index=5*/s32[]{:T(128)}) %tuple.1855), condition=%wide.region_22.23_spmd.clone.clone, body=%wide.region_21.22_spmd.clone.clone.sunk | while | flops 4292 | bytes 19003 | solution.py:60
  1139.2 43.6 %while.682 = (s32[]{:T(128)}, f32[32,32]{1,0:T(8,128)S(1)}, f32[32,32]{1,0:T(8,128)S(1)}, f32[32,32]{0,1:T(8,128)S(1)}, s32[]{:T(128)}, /*index=5*/s32[]{:T(128)}, s32[]{:T(128)}) while((s32[]{:T(128)}, f32[32,32]{1,0:T(8,128)S(1)}, f32[32,32]{1,0:T(8,128)S(1)}, f32[32,32]{0,1:T(8,128)S(1)}, s32[]{:T(128)}, ...), condition=%wide.region_24.25_spmd.clone.clone, body=%wide.region_23.24_spmd.clone.clone.sunk | while | flops 4228 | bytes 18367 | solution.py:78
  1183.8 45.0 %while.683 = (s32[]{:T(128)}, f32[32,32]{0,1:T(8,128)S(1)}, f32[32,32]{0,1:T(8,128)S(1)}, s32[]{:T(128)}, s32[]{:T(128)}, /*index=5*/s32[]{:T(128)}) while((s32[]{:T(128)}, f32[32,32]{0,1:T(8,128)S(1)}, f32[32,32]{0,1:T(8,128)S(1)}, s32[]{:T(128)}, s32[]{:T(128)}, /*index=5*/s32[]{:T(128)}) %tuple.1854), condition=%wide.region_26.27_spmd.clone.clone, body=%wide.region_25.26_spmd.clone.clone.sunk | while | flops 4292 | bytes 19003 | solution.py:60
  1228.8 43.6 %while.684 = (s32[]{:T(128)}, f32[32,32]{1,0:T(8,128)S(1)}, f32[32,32]{1,0:T(8,128)S(1)}, f32[32,32]{0,1:T(8,128)S(1)}, s32[]{:T(128)}, /*index=5*/s32[]{:T(128)}, s32[]{:T(128)}) while((s32[]{:T(128)}, f32[32,32]{1,0:T(8,128)S(1)}, f32[32,32]{1,0:T(8,128)S(1)}, f32[32,32]{0,1:T(8,128)S(1)}, s32[]{:T(128)}, ...), condition=%wide.region_28.29_spmd.clone.clone, body=%wide.region_27.28_spmd.clone.clone.sunk | while | flops 4228 | bytes 18367 | solution.py:78
  1273.3 45.0 %while.685 = (s32[]{:T(128)}, f32[32,32]{0,1:T(8,128)S(1)}, f32[32,32]{0,1:T(8,128)S(1)}, s32[]{:T(128)}, s32[]{:T(128)}, /*index=5*/s32[]{:T(128)}) while((s32[]{:T(128)}, f32[32,32]{0,1:T(8,128)S(1)}, f32[32,32]{0,1:T(8,128)S(1)}, s32[]{:T(128)}, s32[]{:T(128)}, /*index=5*/s32[]{:T(128)}) %tuple.1853), condition=%wide.region_30.31_spmd.clone.clone, body=%wide.region_29.30_spmd.clone.clone.sunk | while | flops 4292 | bytes 19003 | solution.py:60
  1326.6 43.6 %while.686 = (s32[]{:T(128)}, f32[32,32]{1,0:T(8,128)S(1)}, f32[32,32]{1,0:T(8,128)S(1)}, f32[32,32]{0,1:T(8,128)S(1)}, s32[]{:T(128)}, /*index=5*/s32[]{:T(128)}, s32[]{:T(128)}) while((s32[]{:T(128)}, f32[32,32]{1,0:T(8,128)S(1)}, f32[32,32]{1,0:T(8,128)S(1)}, f32[32,32]{0,1:T(8,128)S(1)}, s32[]{:T(128)}, ...), condition=%wide.region_32.33_spmd.clone.clone, body=%wide.region_31.32_spmd.clone.clone.sunk | while | flops 4228 | bytes 18367 | solution.py:78
  1371.0 45.0 %while.687 = (s32[]{:T(128)}, f32[32,32]{0,1:T(8,128)S(1)}, f32[32,32]{0,1:T(8,128)S(1)}, s32[]{:T(128)}, s32[]{:T(128)}, /*index=5*/s32[]{:T(128)}) while((s32[]{:T(128)}, f32[32,32]{0,1:T(8,128)S(1)}, f32[32,32]{0,1:T(8,128)S(1)}, s32[]{:T(128)}, s32[]{:T(128)}, /*index=5*/s32[]{:T(128)}) %tuple.1789), condition=%wide.region_34.35_spmd.clone.clone, body=%wide.region_33.34_spmd.clone.clone.sunk | while | flops 4292 | bytes 19003 | solution.py:60
  1416.1 43.6 %while.688 = (s32[]{:T(128)}, f32[32,32]{1,0:T(8,128)S(1)}, f32[32,32]{1,0:T(8,128)S(1)}, f32[32,32]{0,1:T(8,128)S(1)}, s32[]{:T(128)}, /*index=5*/s32[]{:T(128)}, s32[]{:T(128)}) while((s32[]{:T(128)}, f32[32,32]{1,0:T(8,128)S(1)}, f32[32,32]{1,0:T(8,128)S(1)}, f32[32,32]{0,1:T(8,128)S(1)}, s32[]{:T(128)}, ...), condition=%wide.region_36.37_spmd.clone.clone, body=%wide.region_35.36_spmd.clone.clone.sunk | while | flops 4228 | bytes 18367 | solution.py:78
  1460.5 45.0 %while.689 = (s32[]{:T(128)}, f32[32,32]{0,1:T(8,128)S(1)}, f32[32,32]{0,1:T(8,128)S(1)}, s32[]{:T(128)}, s32[]{:T(128)}, /*index=5*/s32[]{:T(128)}) while((s32[]{:T(128)}, f32[32,32]{0,1:T(8,128)S(1)}, f32[32,32]{0,1:T(8,128)S(1)}, s32[]{:T(128)}, s32[]{:T(128)}, /*index=5*/s32[]{:T(128)}) %tuple.1795), condition=%wide.region_38.39_spmd.clone.clone, body=%wide.region_37.38_spmd.clone.clone.sunk | while | flops 4292 | bytes 19003 | solution.py:60
  1505.5 43.6 %while.690 = (s32[]{:T(128)}, f32[32,32]{1,0:T(8,128)S(1)}, f32[32,32]{1,0:T(8,128)S(1)}, f32[32,32]{0,1:T(8,128)S(1)}, s32[]{:T(128)}, /*index=5*/s32[]{:T(128)}, s32[]{:T(128)}) while((s32[]{:T(128)}, f32[32,32]{1,0:T(8,128)S(1)}, f32[32,32]{1,0:T(8,128)S(1)}, f32[32,32]{0,1:T(8,128)S(1)}, s32[]{:T(128)}, ...), condition=%wide.region_40.41_spmd.clone.clone, body=%wide.region_39.40_spmd.clone.clone.sunk | while | flops 4228 | bytes 18367 | solution.py:78
  1549.8 45.0 %while.691 = (s32[]{:T(128)}, f32[32,32]{0,1:T(8,128)S(1)}, f32[32,32]{0,1:T(8,128)S(1)}, s32[]{:T(128)}, s32[]{:T(128)}, /*index=5*/s32[]{:T(128)}) while((s32[]{:T(128)}, f32[32,32]{0,1:T(8,128)S(1)}, f32[32,32]{0,1:T(8,128)S(1)}, s32[]{:T(128)}, s32[]{:T(128)}, /*index=5*/s32[]{:T(128)}) %tuple.1801), condition=%wide.region_42.43_spmd.clone.clone, body=%wide.region_41.42_spmd.clone.clone.sunk | while | flops 4292 | bytes 19003 | solution.py:60
  1594.9 43.6 %while.692 = (s32[]{:T(128)}, f32[32,32]{1,0:T(8,128)S(1)}, f32[32,32]{1,0:T(8,128)S(1)}, f32[32,32]{0,1:T(8,128)S(1)}, s32[]{:T(128)}, /*index=5*/s32[]{:T(128)}, s32[]{:T(128)}) while((s32[]{:T(128)}, f32[32,32]{1,0:T(8,128)S(1)}, f32[32,32]{1,0:T(8,128)S(1)}, f32[32,32]{0,1:T(8,128)S(1)}, s32[]{:T(128)}, ...), condition=%wide.region_44.45_spmd.clone.clone, body=%wide.region_43.44_spmd.clone.clone.sunk | while | flops 4228 | bytes 18367 | solution.py:78
  1639.2 45.0 %while.693 = (s32[]{:T(128)}, f32[32,32]{0,1:T(8,128)S(1)}, f32[32,32]{0,1:T(8,128)S(1)}, s32[]{:T(128)}, s32[]{:T(128)}, /*index=5*/s32[]{:T(128)}) while((s32[]{:T(128)}, f32[32,32]{0,1:T(8,128)S(1)}, f32[32,32]{0,1:T(8,128)S(1)}, s32[]{:T(128)}, s32[]{:T(128)}, /*index=5*/s32[]{:T(128)}) %tuple.1807), condition=%wide.region_46.47_spmd.clone.clone, body=%wide.region_45.46_spmd.clone.clone.sunk | while | flops 4292 | bytes 19003 | solution.py:60
  1691.8 43.6 %while.694 = (s32[]{:T(128)}, f32[32,32]{1,0:T(8,128)S(1)}, f32[32,32]{1,0:T(8,128)S(1)}, f32[32,32]{0,1:T(8,128)S(1)}, s32[]{:T(128)}, /*index=5*/s32[]{:T(128)}, s32[]{:T(128)}) while((s32[]{:T(128)}, f32[32,32]{1,0:T(8,128)S(1)}, f32[32,32]{1,0:T(8,128)S(1)}, f32[32,32]{0,1:T(8,128)S(1)}, s32[]{:T(128)}, ...), condition=%wide.region_48.49_spmd.clone.clone, body=%wide.region_47.48_spmd.clone.clone.sunk | while | flops 4228 | bytes 18367 | solution.py:78
  1736.0 45.0 %while.695 = (s32[]{:T(128)}, f32[32,32]{0,1:T(8,128)S(1)}, f32[32,32]{0,1:T(8,128)S(1)}, s32[]{:T(128)}, s32[]{:T(128)}, /*index=5*/s32[]{:T(128)}) while((s32[]{:T(128)}, f32[32,32]{0,1:T(8,128)S(1)}, f32[32,32]{0,1:T(8,128)S(1)}, s32[]{:T(128)}, s32[]{:T(128)}, /*index=5*/s32[]{:T(128)}) %tuple.1813), condition=%wide.region_50.51_spmd.clone.clone, body=%wide.region_49.50_spmd.clone.clone.sunk | while | flops 4292 | bytes 19003 | solution.py:60
  1781.0 43.6 %while.696 = (s32[]{:T(128)}, f32[32,32]{1,0:T(8,128)S(1)}, f32[32,32]{1,0:T(8,128)S(1)}, f32[32,32]{0,1:T(8,128)S(1)}, s32[]{:T(128)}, /*index=5*/s32[]{:T(128)}, s32[]{:T(128)}) while((s32[]{:T(128)}, f32[32,32]{1,0:T(8,128)S(1)}, f32[32,32]{1,0:T(8,128)S(1)}, f32[32,32]{0,1:T(8,128)S(1)}, s32[]{:T(128)}, ...), condition=%wide.region_52.53_spmd.clone.clone, body=%wide.region_51.52_spmd.clone.clone.sunk | while | flops 4228 | bytes 18367 | solution.py:78
  1825.1 45.0 %while.697 = (s32[]{:T(128)}, f32[32,32]{0,1:T(8,128)S(1)}, f32[32,32]{0,1:T(8,128)S(1)}, s32[]{:T(128)}, s32[]{:T(128)}, /*index=5*/s32[]{:T(128)}) while((s32[]{:T(128)}, f32[32,32]{0,1:T(8,128)S(1)}, f32[32,32]{0,1:T(8,128)S(1)}, s32[]{:T(128)}, s32[]{:T(128)}, /*index=5*/s32[]{:T(128)}) %tuple.1819), condition=%wide.region_54.55_spmd.clone.clone, body=%wide.region_53.54_spmd.clone.clone.sunk | while | flops 4292 | bytes 19003 | solution.py:60
  1870.2 43.6 %while.698 = (s32[]{:T(128)}, f32[32,32]{1,0:T(8,128)S(1)}, f32[32,32]{1,0:T(8,128)S(1)}, f32[32,32]{0,1:T(8,128)S(1)}, s32[]{:T(128)}, /*index=5*/s32[]{:T(128)}, s32[]{:T(128)}) while((s32[]{:T(128)}, f32[32,32]{1,0:T(8,128)S(1)}, f32[32,32]{1,0:T(8,128)S(1)}, f32[32,32]{0,1:T(8,128)S(1)}, s32[]{:T(128)}, ...), condition=%wide.region_56.57_spmd.clone.clone, body=%wide.region_55.56_spmd.clone.clone.sunk | while | flops 4228 | bytes 18367 | solution.py:78
  1914.3 45.0 %while.699 = (s32[]{:T(128)}, f32[32,32]{0,1:T(8,128)S(1)}, f32[32,32]{0,1:T(8,128)S(1)}, s32[]{:T(128)}, s32[]{:T(128)}, /*index=5*/s32[]{:T(128)}) while((s32[]{:T(128)}, f32[32,32]{0,1:T(8,128)S(1)}, f32[32,32]{0,1:T(8,128)S(1)}, s32[]{:T(128)}, s32[]{:T(128)}, /*index=5*/s32[]{:T(128)}) %tuple.1825), condition=%wide.region_58.59_spmd.clone.clone, body=%wide.region_57.58_spmd.clone.clone.sunk | while | flops 4292 | bytes 19003 | solution.py:60
  1959.4 43.6 %while.700 = (s32[]{:T(128)}, f32[32,32]{1,0:T(8,128)S(1)}, f32[32,32]{1,0:T(8,128)S(1)}, f32[32,32]{0,1:T(8,128)S(1)}, s32[]{:T(128)}, /*index=5*/s32[]{:T(128)}, s32[]{:T(128)}) while((s32[]{:T(128)}, f32[32,32]{1,0:T(8,128)S(1)}, f32[32,32]{1,0:T(8,128)S(1)}, f32[32,32]{0,1:T(8,128)S(1)}, s32[]{:T(128)}, ...), condition=%wide.region_60.61_spmd.clone.clone, body=%wide.region_59.60_spmd.clone.clone.sunk | while | flops 4228 | bytes 18367 | solution.py:78
  2016.5 45.0 %while.701 = (s32[]{:T(128)}, f32[32,32]{0,1:T(8,128)S(1)}, f32[32,32]{0,1:T(8,128)S(1)}, s32[]{:T(128)}, s32[]{:T(128)}, /*index=5*/s32[]{:T(128)}) while((s32[]{:T(128)}, f32[32,32]{0,1:T(8,128)S(1)}, f32[32,32]{0,1:T(8,128)S(1)}, s32[]{:T(128)}, s32[]{:T(128)}, /*index=5*/s32[]{:T(128)}) %tuple.1857), condition=%wide.region_62.63_spmd.clone.clone, body=%wide.region_61.62_spmd.clone.clone.sunk | while | flops 4292 | bytes 19003 | solution.py:60
  2061.5 43.6 %while.702 = (s32[]{:T(128)}, f32[32,32]{1,0:T(8,128)S(1)}, f32[32,32]{1,0:T(8,128)S(1)}, f32[32,32]{0,1:T(8,128)S(1)}, s32[]{:T(128)}, /*index=5*/s32[]{:T(128)}, s32[]{:T(128)}) while((s32[]{:T(128)}, f32[32,32]{1,0:T(8,128)S(1)}, f32[32,32]{1,0:T(8,128)S(1)}, f32[32,32]{0,1:T(8,128)S(1)}, s32[]{:T(128)}, ...), condition=%wide.region_64.65_spmd.clone.clone, body=%wide.region_63.64_spmd.clone.clone.sunk | while | flops 4228 | bytes 18367 | solution.py:78
  (5422 shorter events, 1197.8 us)
Async XLA Ops:
  7.2 538.7 %all-reduce.4.cloned.1.call-start = ((), (), s32[]{:S(2)}) async-start(), calls=%async_computation.1 | async-start | bytes 4194304 | tf_op jit(solution)/shard_map/psum | solution.py:159
  8.1 5.4 collective-permute-start
  12.1 4.4 collective-permute-start.1
  62.1 1.3 copy-start.15
  66.1 0.7 copy-start.24
  66.1 1.6 copy-start.16
  66.1 573.3 %copy-start = (f32[32,32]{1,0:T(8,128)}, f32[32,32]{1,0:T(8,128)S(1)}, u32[]{:S(2)}) copy-start(f32[32,32]{1,0:T(8,128)S(1)} %fusion.258) | copy-start | bytes 12292
  639.5 135.1 %copy-start.2 = (f32[32,32]{1,0:T(8,128)S(1)}, f32[32,32]{1,0:T(8,128)}, u32[]{:S(2)}) copy-start(f32[32,32]{1,0:T(8,128)} %copy-done) | copy-start | bytes 12292
  728.2 91.3 %copy-start.22 = (f32[32,32]{0,1:T(8,128)}, f32[32,32]{0,1:T(8,128)S(1)}, u32[]{:S(2)}) copy-start(f32[32,32]{0,1:T(8,128)S(1)} %get-tuple-element.7857) | copy-start | bytes 12292
  818.2 1.4 copy-start.21
  818.6 98.3 %copy-start.3 = (f32[32,32]{1,0:T(8,128)S(1)}, f32[32,32]{1,0:T(8,128)}, u32[]{:S(2)}) copy-start(f32[32,32]{1,0:T(8,128)} %copy-done) | copy-start | bytes 12292
  819.6 184.9 %copy-start.20 = (f32[32,32]{0,1:T(8,128)S(1)}, f32[32,32]{0,1:T(8,128)}, u32[]{:S(2)}) copy-start(f32[32,32]{0,1:T(8,128)} %custom-call.8) | copy-start | bytes 12292
  906.2 143.3 %copy-start.4 = (f32[32,32]{1,0:T(8,128)S(1)}, f32[32,32]{1,0:T(8,128)}, u32[]{:S(2)}) copy-start(f32[32,32]{1,0:T(8,128)} %copy-done) | copy-start | bytes 12292
  1003.3 90.8 %copy-start.19 = (f32[32,32]{0,1:T(8,128)S(1)}, f32[32,32]{0,1:T(8,128)}, u32[]{:S(2)}) copy-start(f32[32,32]{0,1:T(8,128)} %custom-call.10) | copy-start | bytes 12292
  1003.7 135.5 %copy-start.5 = (f32[32,32]{1,0:T(8,128)S(1)}, f32[32,32]{1,0:T(8,128)}, u32[]{:S(2)}) copy-start(f32[32,32]{1,0:T(8,128)} %copy-done) | copy-start | bytes 12292
  1093.1 90.7 %copy-start.18 = (f32[32,32]{0,1:T(8,128)S(1)}, f32[32,32]{0,1:T(8,128)}, u32[]{:S(2)}) copy-start(f32[32,32]{0,1:T(8,128)} %custom-call.12) | copy-start | bytes 12292
  1093.4 135.4 %copy-start.6 = (f32[32,32]{1,0:T(8,128)S(1)}, f32[32,32]{1,0:T(8,128)}, u32[]{:S(2)}) copy-start(f32[32,32]{1,0:T(8,128)} %copy-done) | copy-start | bytes 12292
  1139.2 134.2 %copy-start.17 = (f32[32,32]{0,1:T(8,128)S(1)}, f32[32,32]{0,1:T(8,128)}, u32[]{:S(2)}) copy-start(f32[32,32]{0,1:T(8,128)} %custom-call.14) | copy-start | bytes 12292
  1183.0 143.6 %copy-start.7 = (f32[32,32]{1,0:T(8,128)S(1)}, f32[32,32]{1,0:T(8,128)}, u32[]{:S(2)}) copy-start(f32[32,32]{1,0:T(8,128)} %copy-done) | copy-start | bytes 12292
  1272.7 143.4 %copy-start.8 = (f32[32,32]{1,0:T(8,128)S(1)}, f32[32,32]{1,0:T(8,128)}, u32[]{:S(2)}) copy-start(f32[32,32]{1,0:T(8,128)} %copy-done) | copy-start | bytes 12292
  1322.9 182.6 %copy-start.9 = (f32[32,32]{1,0:T(8,128)S(1)}, f32[32,32]{1,0:T(8,128)}, u32[]{:S(2)}) copy-start(f32[32,32]{1,0:T(8,128)} %copy-done) | copy-start | bytes 12292
  1371.0 223.8 %copy-start.10 = (f32[32,32]{1,0:T(8,128)S(1)}, f32[32,32]{1,0:T(8,128)}, u32[]{:S(2)}) copy-start(f32[32,32]{1,0:T(8,128)} %copy-done) | copy-start | bytes 12292
  1505.5 186.3 %copy-start.11 = (f32[32,32]{1,0:T(8,128)S(1)}, f32[32,32]{1,0:T(8,128)}, u32[]{:S(2)}) copy-start(f32[32,32]{1,0:T(8,128)} %copy-done) | copy-start | bytes 12292
  1549.8 231.2 %copy-start.12 = (f32[32,32]{1,0:T(8,128)S(1)}, f32[32,32]{1,0:T(8,128)}, u32[]{:S(2)}) copy-start(f32[32,32]{1,0:T(8,128)} %copy-done) | copy-start | bytes 12292
  1638.7 231.5 %copy-start.13 = (f32[32,32]{1,0:T(8,128)S(1)}, f32[32,32]{1,0:T(8,128)}, u32[]{:S(2)}) copy-start(f32[32,32]{1,0:T(8,128)} %copy-done) | copy-start | bytes 12292
  1691.8 267.6 %copy-start.14 = (f32[32,32]{1,0:T(8,128)S(1)}, f32[32,32]{1,0:T(8,128)}, u32[]{:S(2)}) copy-start(f32[32,32]{1,0:T(8,128)} %copy-done) | copy-start | bytes 12292
  1913.8 102.7 %copy-start.23 = (f32[32,32]{0,1:T(8,128)S(1)}, f32[32,32]{0,1:T(8,128)}, u32[]{:S(2)}) copy-start(f32[32,32]{0,1:T(8,128)} %custom-call.30) | copy-start | bytes 12292
  1959.4 102.1 %copy-start.1 = (f32[32,32]{1,0:T(8,128)S(1)}, f32[32,32]{1,0:T(8,128)}, u32[]{:S(2)}) copy-start(f32[32,32]{1,0:T(8,128)} %copy-done) | copy-start | bytes 12292
  2133.2 0.7 copy-start.25
Sparse Core Ops, SparseCore 0:
  66.2 479.6 all-reduce.3
where the time goes:
time: 2160 us; the launch traced here: 2140 us
  local copies, waits for them, and re-layouts  667 us (31%)
  other arithmetic  500 us (23%)
  loops' own time  382 us (18%)
  waiting for transfers between devices  371 us (17%)
  blocking collectives  144 us (7%)
  matrix products  56.1 us (3%)
    another operation x16, loops' own time, small_factor(): lax.fori_loop(0, order, column_step, (matrix, jnp.zeros_like(matrix)))[1]  369 us
    psum x1, waiting for transfers between devices, shards(): gram_block, projected = lax.psum((gram_block, projected), ('rows', 'cols'))  368 us
    mul x1024, other arithmetic, row_step(): rest = rest - below[:, None] * value  363 us
    dynamic_slice x512, local copies, waits for them, and re-layouts, row_step(): pivot = lax.dynamic_slice_in_dim(column, index_row, 1, 0)[0]  322 us
    dynamic_slice x512, local copies, waits for them, and re-layouts, column_step(): pivot = jnp.sqrt(lax.dynamic_slice_in_dim(column, index_col, 1, 0)[0])  301 us
    psum x1, blocking collectives, shards(): gram_block, projected = lax.psum((gram_block, projected), ('rows', 'cols'))  110 us
    select_n x512, other arithmetic, column_step(): lower = jnp.where(positions[None, :] == index_col, column[:, None], lower)  80.9 us
    dot_general x123, matrix products, matmul(): jnp.dot(left, right, precision=lax.Precision.HIGHEST, preferred_element_t...  46.5 us

commit v1 on v0

--- a/solution.py
+++ b/solution.py
@@ -156,7 +156,7 @@
         leading, row_major, (((0,), (0,)), ((), ())), preferred_element_type=jnp.float32
     )
     projected = jnp.dot(grad_part, leading, preferred_element_type=jnp.float32)
-    gram_block, projected = lax.psum((gram_block, projected), ("rows", "cols"))
+    gram_block, projected = lax.psum(lax.psum((gram_block, projected), "rows"), "cols")
     gram_head = gram_block[:, :factored]
     gram_own = lax.dynamic_slice_in_dim(
         gram_block, lax.axis_index("cols") * cols_here, cols_here, 1

time: 2160 us -> 2110 us (0.977)
  waiting for transfers between devices: 371 us -> 276 us
  blocking collectives: 144 us -> 197 us
    psum x1 -> x2, waiting for transfers between devices: 368 us -> 273 us  [the longest x1 273 us: shards(): lax.psum((gram_block, projected), 'rows')]
    psum x1 -> x2, blocking collectives: 110 us -> 162 us  [the longest x1 113 us: shards(): lax.psum((gram_block, projected), 'rows')]
where the time goes in v1:
time: 2110 us; the launch traced here: 2100 us
  local copies, waits for them, and re-layouts  667 us (32%)
  other arithmetic  500 us (24%)
  loops' own time  383 us (18%)
  waiting for transfers between devices  276 us (13%)
  blocking collectives  197 us (9%)
  matrix products  56.1 us (3%)
    another operation x16, loops' own time, small_factor(): lax.fori_loop(0, order, column_step, (matrix, jnp.zeros_like(matrix)))[1]  370 us
    mul x1024, other arithmetic, row_step(): rest = rest - below[:, None] * value  363 us
    dynamic_slice x512, local copies, waits for them, and re-layouts, row_step(): pivot = lax.dynamic_slice_in_dim(column, index_row, 1, 0)[0]  322 us
    dynamic_slice x512, local copies, waits for them, and re-layouts, column_step(): pivot = jnp.sqrt(lax.dynamic_slice_in_dim(column, index_col, 1, 0)[0])  302 us
    psum x1, waiting for transfers between devices, shards(): lax.psum((gram_block, projected), 'rows')  273 us
    psum x1, blocking collectives, shards(): lax.psum((gram_block, projected), 'rows')  113 us
    select_n x512, other arithmetic, column_step(): lower = jnp.where(positions[None, :] == index_col, column[:, None], lower)  80.8 us
    psum x1, blocking collectives, shards(): lax.psum(lax.psum((gram_block, projected), 'rows'), 'cols')  49.8 us

profile of v1, /device:TPU:1, one launch (start us, length us, event | category | flops | bytes accessed | tf_op | source)
XLA Modules:
  0.0 2099.4 jit_solution(10871177124091725457)
XLA Ops:
  8.1 4.0 collective-permute-start
  13.5 2.9 collective-permute-done.1
  18.4 6.7 fusion.98
  25.0 2.9 copy.37
  27.9 34.2 %all_to_all.19 = bf16[8,1024,128]{1,2,0:T(8,128)(2,1)S(1)} all-to-all(bf16[8,1024,128]{1,2,0:T(8,128)(2,1)S(1)} %copy.37), channel_id=1, replica_groups=mesh['rows'=64,'cols'=8] {'cols'}, dimensions={0} | all-to-all | bytes 4194304 | tf_op jit(solution)/shard_map/all_to_all | solution.py:149
  63.4 2.6 fusion.161
  66.1 272.9 %all-reduce.5.cloned.1.call-done = f32[512,1024]{1,0:T(8,128)} async-done(((f32[512,1024]{1,0:T(8,128)}), f32[512,1024]{1,0:T(8,128)}) %all-reduce.5.cloned.1.call-update) | async-done | bytes 2097168 | tf_op jit(solution)/shard_map/psum | solution.py:159
  339.8 112.5 %psum.30 = f32[512]{0:T(512)S(1)} all-reduce(f32[512]{0:T(512)S(1)} %bitcast.1236), channel_id=1, replica_groups=mesh['rows'=64,'cols'=8] {'rows'}, use_global_device_ids=true, to_apply=%region_66.67 | all-reduce | flops 512 | bytes 4096 | tf_op jit(solution)/shard_map/psum | solution.py:159
  452.4 49.8 %psum.31 = f32[512]{0:T(512)S(1)} all-reduce(f32[512]{0:T(512)S(1)} %psum.30), channel_id=1, replica_groups=mesh['rows'=64,'cols'=8] {'cols'}, use_global_device_ids=true, to_apply=%region_67.68 | all-reduce | flops 512 | bytes 4096 | tf_op jit(solution)/shard_map/psum | solution.py:159
  503.0 47.9 %while.671 = (s32[]{:T(128)}, f32[32,32]{0,1:T(8,128)S(1)}, f32[32,32]{0,1:T(8,128)S(1)}, s32[]{:T(128)}, s32[]{:T(128)}, /*index=5*/s32[]{:T(128)}) while((s32[]{:T(128)}, f32[32,32]{0,1:T(8,128)S(1)}, f32[32,32]{0,1:T(8,128)S(1)}, s32[]{:T(128)}, s32[]{:T(128)}, /*index=5*/s32[]{:T(128)}) %tuple.1741), condition=%wide.region_3.4_spmd.clone.clone, body=%wide.region_2.3_spmd.clone.clone.sunk | while | flops 4292 | bytes 19003 | solution.py:60
  550.9 43.6 %while.672 = (s32[]{:T(128)}, f32[32,32]{1,0:T(8,128)S(1)}, f32[32,32]{1,0:T(8,128)S(1)}, f32[32,32]{0,1:T(8,128)S(1)}, s32[]{:T(128)}, /*index=5*/s32[]{:T(128)}, s32[]{:T(128)}) while((s32[]{:T(128)}, f32[32,32]{1,0:T(8,128)S(1)}, f32[32,32]{1,0:T(8,128)S(1)}, f32[32,32]{0,1:T(8,128)S(1)}, s32[]{:T(128)}, ...), condition=%wide.region_5.6_spmd.clone.clone, body=%wide.region_4.5_spmd.clone.clone.sunk | while | flops 4228 | bytes 18367 | solution.py:78
  595.9 2.3 convolution_subtract_fusion
  598.3 45.0 %while.673 = (s32[]{:T(128)}, f32[32,32]{0,1:T(8,128)S(1)}, f32[32,32]{0,1:T(8,128)S(1)}, s32[]{:T(128)}, s32[]{:T(128)}, /*index=5*/s32[]{:T(128)}) while((s32[]{:T(128)}, f32[32,32]{0,1:T(8,128)S(1)}, f32[32,32]{0,1:T(8,128)S(1)}, s32[]{:T(128)}, s32[]{:T(128)}, /*index=5*/s32[]{:T(128)}) %tuple.1747), condition=%wide.region_7.8_spmd.clone.clone, body=%wide.region_6.7_spmd.clone.clone.sunk | while | flops 4292 | bytes 19003 | solution.py:60
  643.3 43.6 %while.674 = (s32[]{:T(128)}, f32[32,32]{1,0:T(8,128)S(1)}, f32[32,32]{1,0:T(8,128)S(1)}, f32[32,32]{0,1:T(8,128)S(1)}, s32[]{:T(128)}, /*index=5*/s32[]{:T(128)}, s32[]{:T(128)}) while((s32[]{:T(128)}, f32[32,32]{1,0:T(8,128)S(1)}, f32[32,32]{1,0:T(8,128)S(1)}, f32[32,32]{0,1:T(8,128)S(1)}, s32[]{:T(128)}, ...), condition=%wide.region_9.10_spmd.clone.clone, body=%wide.region_8.9_spmd.clone.clone.sunk | while | flops 4228 | bytes 18367 | solution.py:78
  688.3 45.0 %while.675 = (s32[]{:T(128)}, f32[32,32]{0,1:T(8,128)S(1)}, f32[32,32]{0,1:T(8,128)S(1)}, s32[]{:T(128)}, s32[]{:T(128)}, /*index=5*/s32[]{:T(128)}) while((s32[]{:T(128)}, f32[32,32]{0,1:T(8,128)S(1)}, f32[32,32]{0,1:T(8,128)S(1)}, s32[]{:T(128)}, s32[]{:T(128)}, /*index=5*/s32[]{:T(128)}) %tuple.1753), condition=%wide.region_11.12_spmd.clone.clone, body=%wide.region_10.11_spmd.clone.clone.sunk | while | flops 4292 | bytes 19003 | solution.py:60
  733.3 43.6 %while.676 = (s32[]{:T(128)}, f32[32,32]{1,0:T(8,128)S(1)}, f32[32,32]{1,0:T(8,128)S(1)}, f32[32,32]{0,1:T(8,128)S(1)}, s32[]{:T(128)}, /*index=5*/s32[]{:T(128)}, s32[]{:T(128)}) while((s32[]{:T(128)}, f32[32,32]{1,0:T(8,128)S(1)}, f32[32,32]{1,0:T(8,128)S(1)}, f32[32,32]{0,1:T(8,128)S(1)}, s32[]{:T(128)}, ...), condition=%wide.region_13.14_spmd.clone.clone, body=%wide.region_12.13_spmd.clone.clone.sunk | while | flops 4228 | bytes 18367 | solution.py:78
  778.3 86.5 %while.677 = (s32[]{:T(128)}, f32[32,32]{0,1:T(8,128)S(1)}, f32[32,32]{0,1:T(8,128)}, s32[]{:T(128)}, s32[]{:T(128)}, /*index=5*/s32[]{:T(128)}) while((s32[]{:T(128)}, f32[32,32]{0,1:T(8,128)S(1)}, f32[32,32]{0,1:T(8,128)}, s32[]{:T(128)}, s32[]{:T(128)}, /*index=5*/s32[]{:T(128)}) %tuple.1759), condition=%wide.region_15.16_spmd.clone.clone, body=%wide.region_14.15_spmd.clone.clone.sunk | while | flops 4292 | bytes 19003 | solution.py:60
  865.0 1.4 scatter.101
  866.4 2.1 scatter.104
  868.5 1.4 scatter.105
  869.9 2.1 scatter.106
  872.0 1.4 scatter.109
  873.5 2.1 scatter.110
  875.6 86.4 %while.678 = (s32[]{:T(128)}, f32[32,32]{1,0:T(8,128)S(1)}, f32[32,32]{1,0:T(8,128)S(1)}, f32[32,32]{0,1:T(8,128)}, s32[]{:T(128)}, /*index=5*/s32[]{:T(128)}, s32[]{:T(128)}) while((s32[]{:T(128)}, f32[32,32]{1,0:T(8,128)S(1)}, f32[32,32]{1,0:T(8,128)S(1)}, f32[32,32]{0,1:T(8,128)}, s32[]{:T(128)}, ...), condition=%wide.region_17.18_spmd.clone.clone, body=%wide.region_16.17_spmd.clone.clone.sunk | while | flops 4228 | bytes 18751 | solution.py:78
  963.1 45.0 %while.679 = (s32[]{:T(128)}, f32[32,32]{0,1:T(8,128)S(1)}, f32[32,32]{0,1:T(8,128)S(1)}, s32[]{:T(128)}, s32[]{:T(128)}, /*index=5*/s32[]{:T(128)}) while((s32[]{:T(128)}, f32[32,32]{0,1:T(8,128)S(1)}, f32[32,32]{0,1:T(8,128)S(1)}, s32[]{:T(128)}, s32[]{:T(128)}, /*index=5*/s32[]{:T(128)}) %tuple.1858), condition=%wide.region_19.20_spmd.clone.clone, body=%wide.region_18.19_spmd.clone.clone.sunk | while | flops 4292 | bytes 19003 | solution.py:60
  1008.1 43.6 %while.680 = (s32[]{:T(128)}, f32[32,32]{1,0:T(8,128)S(1)}, f32[32,32]{1,0:T(8,128)S(1)}, f32[32,32]{0,1:T(8,128)S(1)}, s32[]{:T(128)}, /*index=5*/s32[]{:T(128)}, s32[]{:T(128)}) while((s32[]{:T(128)}, f32[32,32]{1,0:T(8,128)S(1)}, f32[32,32]{1,0:T(8,128)S(1)}, f32[32,32]{0,1:T(8,128)S(1)}, s32[]{:T(128)}, ...), condition=%wide.region_21.22_spmd.clone.clone, body=%wide.region_20.21_spmd.clone.clone.sunk | while | flops 4228 | bytes 18367 | solution.py:78
  1052.8 45.0 %while.681 = (s32[]{:T(128)}, f32[32,32]{0,1:T(8,128)S(1)}, f32[32,32]{0,1:T(8,128)S(1)}, s32[]{:T(128)}, s32[]{:T(128)}, /*index=5*/s32[]{:T(128)}) while((s32[]{:T(128)}, f32[32,32]{0,1:T(8,128)S(1)}, f32[32,32]{0,1:T(8,128)S(1)}, s32[]{:T(128)}, s32[]{:T(128)}, /*index=5*/s32[]{:T(128)}) %tuple.1857), condition=%wide.region_23.24_spmd.clone.clone, body=%wide.region_22.23_spmd.clone.clone.sunk | while | flops 4292 | bytes 19003 | solution.py:60
  1097.8 43.6 %while.682 = (s32[]{:T(128)}, f32[32,32]{1,0:T(8,128)S(1)}, f32[32,32]{1,0:T(8,128)S(1)}, f32[32,32]{0,1:T(8,128)S(1)}, s32[]{:T(128)}, /*index=5*/s32[]{:T(128)}, s32[]{:T(128)}) while((s32[]{:T(128)}, f32[32,32]{1,0:T(8,128)S(1)}, f32[32,32]{1,0:T(8,128)S(1)}, f32[32,32]{0,1:T(8,128)S(1)}, s32[]{:T(128)}, ...), condition=%wide.region_25.26_spmd.clone.clone, body=%wide.region_24.25_spmd.clone.clone.sunk | while | flops 4228 | bytes 18367 | solution.py:78
  1142.4 45.0 %while.683 = (s32[]{:T(128)}, f32[32,32]{0,1:T(8,128)S(1)}, f32[32,32]{0,1:T(8,128)S(1)}, s32[]{:T(128)}, s32[]{:T(128)}, /*index=5*/s32[]{:T(128)}) while((s32[]{:T(128)}, f32[32,32]{0,1:T(8,128)S(1)}, f32[32,32]{0,1:T(8,128)S(1)}, s32[]{:T(128)}, s32[]{:T(128)}, /*index=5*/s32[]{:T(128)}) %tuple.1856), condition=%wide.region_27.28_spmd.clone.clone, body=%wide.region_26.27_spmd.clone.clone.sunk | while | flops 4292 | bytes 19003 | solution.py:60
  1187.4 43.6 %while.684 = (s32[]{:T(128)}, f32[32,32]{1,0:T(8,128)S(1)}, f32[32,32]{1,0:T(8,128)S(1)}, f32[32,32]{0,1:T(8,128)S(1)}, s32[]{:T(128)}, /*index=5*/s32[]{:T(128)}, s32[]{:T(128)}) while((s32[]{:T(128)}, f32[32,32]{1,0:T(8,128)S(1)}, f32[32,32]{1,0:T(8,128)S(1)}, f32[32,32]{0,1:T(8,128)S(1)}, s32[]{:T(128)}, ...), condition=%wide.region_29.30_spmd.clone.clone, body=%wide.region_28.29_spmd.clone.clone.sunk | while | flops 4228 | bytes 18367 | solution.py:78
  1232.0 45.0 %while.685 = (s32[]{:T(128)}, f32[32,32]{0,1:T(8,128)S(1)}, f32[32,32]{0,1:T(8,128)S(1)}, s32[]{:T(128)}, s32[]{:T(128)}, /*index=5*/s32[]{:T(128)}) while((s32[]{:T(128)}, f32[32,32]{0,1:T(8,128)S(1)}, f32[32,32]{0,1:T(8,128)S(1)}, s32[]{:T(128)}, s32[]{:T(128)}, /*index=5*/s32[]{:T(128)}) %tuple.1855), condition=%wide.region_31.32_spmd.clone.clone, body=%wide.region_30.31_spmd.clone.clone.sunk | while | flops 4292 | bytes 19003 | solution.py:60
  1285.3 43.6 %while.686 = (s32[]{:T(128)}, f32[32,32]{1,0:T(8,128)S(1)}, f32[32,32]{1,0:T(8,128)S(1)}, f32[32,32]{0,1:T(8,128)S(1)}, s32[]{:T(128)}, /*index=5*/s32[]{:T(128)}, s32[]{:T(128)}) while((s32[]{:T(128)}, f32[32,32]{1,0:T(8,128)S(1)}, f32[32,32]{1,0:T(8,128)S(1)}, f32[32,32]{0,1:T(8,128)S(1)}, s32[]{:T(128)}, ...), condition=%wide.region_33.34_spmd.clone.clone, body=%wide.region_32.33_spmd.clone.clone.sunk | while | flops 4228 | bytes 18367 | solution.py:78
  1329.6 45.0 %while.687 = (s32[]{:T(128)}, f32[32,32]{0,1:T(8,128)S(1)}, f32[32,32]{0,1:T(8,128)S(1)}, s32[]{:T(128)}, s32[]{:T(128)}, /*index=5*/s32[]{:T(128)}) while((s32[]{:T(128)}, f32[32,32]{0,1:T(8,128)S(1)}, f32[32,32]{0,1:T(8,128)S(1)}, s32[]{:T(128)}, s32[]{:T(128)}, /*index=5*/s32[]{:T(128)}) %tuple.1789), condition=%wide.region_35.36_spmd.clone.clone, body=%wide.region_34.35_spmd.clone.clone.sunk | while | flops 4292 | bytes 19003 | solution.py:60
  1374.7 43.6 %while.688 = (s32[]{:T(128)}, f32[32,32]{1,0:T(8,128)S(1)}, f32[32,32]{1,0:T(8,128)S(1)}, f32[32,32]{0,1:T(8,128)S(1)}, s32[]{:T(128)}, /*index=5*/s32[]{:T(128)}, s32[]{:T(128)}) while((s32[]{:T(128)}, f32[32,32]{1,0:T(8,128)S(1)}, f32[32,32]{1,0:T(8,128)S(1)}, f32[32,32]{0,1:T(8,128)S(1)}, s32[]{:T(128)}, ...), condition=%wide.region_37.38_spmd.clone.clone, body=%wide.region_36.37_spmd.clone.clone.sunk | while | flops 4228 | bytes 18367 | solution.py:78
  1419.1 45.0 %while.689 = (s32[]{:T(128)}, f32[32,32]{0,1:T(8,128)S(1)}, f32[32,32]{0,1:T(8,128)S(1)}, s32[]{:T(128)}, s32[]{:T(128)}, /*index=5*/s32[]{:T(128)}) while((s32[]{:T(128)}, f32[32,32]{0,1:T(8,128)S(1)}, f32[32,32]{0,1:T(8,128)S(1)}, s32[]{:T(128)}, s32[]{:T(128)}, /*index=5*/s32[]{:T(128)}) %tuple.1795), condition=%wide.region_39.40_spmd.clone.clone, body=%wide.region_38.39_spmd.clone.clone.sunk | while | flops 4292 | bytes 19003 | solution.py:60
  1464.1 43.6 %while.690 = (s32[]{:T(128)}, f32[32,32]{1,0:T(8,128)S(1)}, f32[32,32]{1,0:T(8,128)S(1)}, f32[32,32]{0,1:T(8,128)S(1)}, s32[]{:T(128)}, /*index=5*/s32[]{:T(128)}, s32[]{:T(128)}) while((s32[]{:T(128)}, f32[32,32]{1,0:T(8,128)S(1)}, f32[32,32]{1,0:T(8,128)S(1)}, f32[32,32]{0,1:T(8,128)S(1)}, s32[]{:T(128)}, ...), condition=%wide.region_41.42_spmd.clone.clone, body=%wide.region_40.41_spmd.clone.clone.sunk | while | flops 4228 | bytes 18367 | solution.py:78
  1508.4 45.0 %while.691 = (s32[]{:T(128)}, f32[32,32]{0,1:T(8,128)S(1)}, f32[32,32]{0,1:T(8,128)S(1)}, s32[]{:T(128)}, s32[]{:T(128)}, /*index=5*/s32[]{:T(128)}) while((s32[]{:T(128)}, f32[32,32]{0,1:T(8,128)S(1)}, f32[32,32]{0,1:T(8,128)S(1)}, s32[]{:T(128)}, s32[]{:T(128)}, /*index=5*/s32[]{:T(128)}) %tuple.1801), condition=%wide.region_43.44_spmd.clone.clone, body=%wide.region_42.43_spmd.clone.clone.sunk | while | flops 4292 | bytes 19003 | solution.py:60
  1553.5 43.6 %while.692 = (s32[]{:T(128)}, f32[32,32]{1,0:T(8,128)S(1)}, f32[32,32]{1,0:T(8,128)S(1)}, f32[32,32]{0,1:T(8,128)S(1)}, s32[]{:T(128)}, /*index=5*/s32[]{:T(128)}, s32[]{:T(128)}) while((s32[]{:T(128)}, f32[32,32]{1,0:T(8,128)S(1)}, f32[32,32]{1,0:T(8,128)S(1)}, f32[32,32]{0,1:T(8,128)S(1)}, s32[]{:T(128)}, ...), condition=%wide.region_45.46_spmd.clone.clone, body=%wide.region_44.45_spmd.clone.clone.sunk | while | flops 4228 | bytes 18367 | solution.py:78
  1597.8 45.0 %while.693 = (s32[]{:T(128)}, f32[32,32]{0,1:T(8,128)S(1)}, f32[32,32]{0,1:T(8,128)S(1)}, s32[]{:T(128)}, s32[]{:T(128)}, /*index=5*/s32[]{:T(128)}) while((s32[]{:T(128)}, f32[32,32]{0,1:T(8,128)S(1)}, f32[32,32]{0,1:T(8,128)S(1)}, s32[]{:T(128)}, s32[]{:T(128)}, /*index=5*/s32[]{:T(128)}) %tuple.1807), condition=%wide.region_47.48_spmd.clone.clone, body=%wide.region_46.47_spmd.clone.clone.sunk | while | flops 4292 | bytes 19003 | solution.py:60
  1650.4 43.6 %while.694 = (s32[]{:T(128)}, f32[32,32]{1,0:T(8,128)S(1)}, f32[32,32]{1,0:T(8,128)S(1)}, f32[32,32]{0,1:T(8,128)S(1)}, s32[]{:T(128)}, /*index=5*/s32[]{:T(128)}, s32[]{:T(128)}) while((s32[]{:T(128)}, f32[32,32]{1,0:T(8,128)S(1)}, f32[32,32]{1,0:T(8,128)S(1)}, f32[32,32]{0,1:T(8,128)S(1)}, s32[]{:T(128)}, ...), condition=%wide.region_49.50_spmd.clone.clone, body=%wide.region_48.49_spmd.clone.clone.sunk | while | flops 4228 | bytes 18367 | solution.py:78
  1694.6 45.0 %while.695 = (s32[]{:T(128)}, f32[32,32]{0,1:T(8,128)S(1)}, f32[32,32]{0,1:T(8,128)S(1)}, s32[]{:T(128)}, s32[]{:T(128)}, /*index=5*/s32[]{:T(128)}) while((s32[]{:T(128)}, f32[32,32]{0,1:T(8,128)S(1)}, f32[32,32]{0,1:T(8,128)S(1)}, s32[]{:T(128)}, s32[]{:T(128)}, /*index=5*/s32[]{:T(128)}) %tuple.1813), condition=%wide.region_51.52_spmd.clone.clone, body=%wide.region_50.51_spmd.clone.clone.sunk | while | flops 4292 | bytes 19003 | solution.py:60
  1739.6 43.6 %while.696 = (s32[]{:T(128)}, f32[32,32]{1,0:T(8,128)S(1)}, f32[32,32]{1,0:T(8,128)S(1)}, f32[32,32]{0,1:T(8,128)S(1)}, s32[]{:T(128)}, /*index=5*/s32[]{:T(128)}, s32[]{:T(128)}) while((s32[]{:T(128)}, f32[32,32]{1,0:T(8,128)S(1)}, f32[32,32]{1,0:T(8,128)S(1)}, f32[32,32]{0,1:T(8,128)S(1)}, s32[]{:T(128)}, ...), condition=%wide.region_53.54_spmd.clone.clone, body=%wide.region_52.53_spmd.clone.clone.sunk | while | flops 4228 | bytes 18367 | solution.py:78
  1783.8 45.0 %while.697 = (s32[]{:T(128)}, f32[32,32]{0,1:T(8,128)S(1)}, f32[32,32]{0,1:T(8,128)S(1)}, s32[]{:T(128)}, s32[]{:T(128)}, /*index=5*/s32[]{:T(128)}) while((s32[]{:T(128)}, f32[32,32]{0,1:T(8,128)S(1)}, f32[32,32]{0,1:T(8,128)S(1)}, s32[]{:T(128)}, s32[]{:T(128)}, /*index=5*/s32[]{:T(128)}) %tuple.1819), condition=%wide.region_55.56_spmd.clone.clone, body=%wide.region_54.55_spmd.clone.clone.sunk | while | flops 4292 | bytes 19003 | solution.py:60
  1828.8 43.6 %while.698 = (s32[]{:T(128)}, f32[32,32]{1,0:T(8,128)S(1)}, f32[32,32]{1,0:T(8,128)S(1)}, f32[32,32]{0,1:T(8,128)S(1)}, s32[]{:T(128)}, /*index=5*/s32[]{:T(128)}, s32[]{:T(128)}) while((s32[]{:T(128)}, f32[32,32]{1,0:T(8,128)S(1)}, f32[32,32]{1,0:T(8,128)S(1)}, f32[32,32]{0,1:T(8,128)S(1)}, s32[]{:T(128)}, ...), condition=%wide.region_57.58_spmd.clone.clone, body=%wide.region_56.57_spmd.clone.clone.sunk | while | flops 4228 | bytes 18367 | solution.py:78
  1873.0 45.0 %while.699 = (s32[]{:T(128)}, f32[32,32]{0,1:T(8,128)S(1)}, f32[32,32]{0,1:T(8,128)S(1)}, s32[]{:T(128)}, s32[]{:T(128)}, /*index=5*/s32[]{:T(128)}) while((s32[]{:T(128)}, f32[32,32]{0,1:T(8,128)S(1)}, f32[32,32]{0,1:T(8,128)S(1)}, s32[]{:T(128)}, s32[]{:T(128)}, /*index=5*/s32[]{:T(128)}) %tuple.1825), condition=%wide.region_59.60_spmd.clone.clone, body=%wide.region_58.59_spmd.clone.clone.sunk | while | flops 4292 | bytes 19003 | solution.py:60
  1918.0 43.6 %while.700 = (s32[]{:T(128)}, f32[32,32]{1,0:T(8,128)S(1)}, f32[32,32]{1,0:T(8,128)S(1)}, f32[32,32]{0,1:T(8,128)S(1)}, s32[]{:T(128)}, /*index=5*/s32[]{:T(128)}, s32[]{:T(128)}) while((s32[]{:T(128)}, f32[32,32]{1,0:T(8,128)S(1)}, f32[32,32]{1,0:T(8,128)S(1)}, f32[32,32]{0,1:T(8,128)S(1)}, s32[]{:T(128)}, ...), condition=%wide.region_61.62_spmd.clone.clone, body=%wide.region_60.61_spmd.clone.clone.sunk | while | flops 4228 | bytes 18367 | solution.py:78
  1975.1 45.0 %while.701 = (s32[]{:T(128)}, f32[32,32]{0,1:T(8,128)S(1)}, f32[32,32]{0,1:T(8,128)S(1)}, s32[]{:T(128)}, s32[]{:T(128)}, /*index=5*/s32[]{:T(128)}) while((s32[]{:T(128)}, f32[32,32]{0,1:T(8,128)S(1)}, f32[32,32]{0,1:T(8,128)S(1)}, s32[]{:T(128)}, s32[]{:T(128)}, /*index=5*/s32[]{:T(128)}) %tuple.1859), condition=%wide.region_63.64_spmd.clone.clone, body=%wide.region_62.63_spmd.clone.clone.sunk | while | flops 4292 | bytes 19003 | solution.py:60
  2020.1 43.6 %while.702 = (s32[]{:T(128)}, f32[32,32]{1,0:T(8,128)S(1)}, f32[32,32]{1,0:T(8,128)S(1)}, f32[32,32]{0,1:T(8,128)S(1)}, s32[]{:T(128)}, /*index=5*/s32[]{:T(128)}, s32[]{:T(128)}) while((s32[]{:T(128)}, f32[32,32]{1,0:T(8,128)S(1)}, f32[32,32]{1,0:T(8,128)S(1)}, f32[32,32]{0,1:T(8,128)S(1)}, s32[]{:T(128)}, ...), condition=%wide.region_65.66_spmd.clone.clone, body=%wide.region_64.65_spmd.clone.clone.sunk | while | flops 4228 | bytes 18367 | solution.py:78
  (5426 shorter events, 1199.1 us)
Async XLA Ops:
  7.2 331.9 %all-reduce.5.cloned.1.call-start = ((), (), s32[]{:S(2)}) async-start(), calls=%async_computation.1 | async-start | bytes 4194304 | tf_op jit(solution)/shard_map/psum | solution.py:159
  8.1 5.4 collective-permute-start
  12.1 4.4 collective-permute-start.1
  62.1 1.3 copy-start.15
  66.0 273.4 %copy-start.24 = (bf16[8,1024]{1,0:T(8,128)(2,1)S(1)}, bf16[8,1024]{1,0:T(8,128)(2,1)}, u32[]{:S(2)}) copy-start(bf16[8,1024]{1,0:T(8,128)(2,1)} %param.133) | copy-start | bytes 49156
  66.0 273.4 %copy-start.16 = (bf16[8,1024,128]{1,2,0:T(8,128)(2,1)S(1)}, bf16[8,1024,128]{1,2,0:T(8,128)(2,1)}, u32[]{:S(2)}) copy-start(bf16[8,1024,128]{1,2,0:T(8,128)(2,1)} %copy-done.15) | copy-start | bytes 6291460
  66.1 436.1 %all-reduce.7.cloned.1.call-start = ((), (), s32[]{:S(2)}) async-start(), calls=%async_computation.2 | async-start | bytes 4194304 | tf_op jit(solution)/shard_map/psum | solution.py:159
  339.1 259.1 %copy-start = (f32[32,32]{1,0:T(8,128)}, f32[32,32]{1,0:T(8,128)S(1)}, u32[]{:S(2)}) copy-start(f32[32,32]{1,0:T(8,128)S(1)} %fusion.258) | copy-start | bytes 12292
  598.2 135.1 %copy-start.2 = (f32[32,32]{1,0:T(8,128)S(1)}, f32[32,32]{1,0:T(8,128)}, u32[]{:S(2)}) copy-start(f32[32,32]{1,0:T(8,128)} %copy-done) | copy-start | bytes 12292
  686.9 91.3 %copy-start.22 = (f32[32,32]{0,1:T(8,128)}, f32[32,32]{0,1:T(8,128)S(1)}, u32[]{:S(2)}) copy-start(f32[32,32]{0,1:T(8,128)S(1)} %get-tuple-element.7861) | copy-start | bytes 12292
  776.9 1.4 copy-start.21
  777.3 98.2 %copy-start.3 = (f32[32,32]{1,0:T(8,128)S(1)}, f32[32,32]{1,0:T(8,128)}, u32[]{:S(2)}) copy-start(f32[32,32]{1,0:T(8,128)} %copy-done) | copy-start | bytes 12292
  778.3 184.8 %copy-start.20 = (f32[32,32]{0,1:T(8,128)S(1)}, f32[32,32]{0,1:T(8,128)}, u32[]{:S(2)}) copy-start(f32[32,32]{0,1:T(8,128)} %custom-call.8) | copy-start | bytes 12292
  864.9 143.2 %copy-start.4 = (f32[32,32]{1,0:T(8,128)S(1)}, f32[32,32]{1,0:T(8,128)}, u32[]{:S(2)}) copy-start(f32[32,32]{1,0:T(8,128)} %copy-done) | copy-start | bytes 12292
  962.0 90.8 %copy-start.19 = (f32[32,32]{0,1:T(8,128)S(1)}, f32[32,32]{0,1:T(8,128)}, u32[]{:S(2)}) copy-start(f32[32,32]{0,1:T(8,128)} %custom-call.10) | copy-start | bytes 12292
  962.3 135.5 %copy-start.5 = (f32[32,32]{1,0:T(8,128)S(1)}, f32[32,32]{1,0:T(8,128)}, u32[]{:S(2)}) copy-start(f32[32,32]{1,0:T(8,128)} %copy-done) | copy-start | bytes 12292
  1051.7 90.7 %copy-start.18 = (f32[32,32]{0,1:T(8,128)S(1)}, f32[32,32]{0,1:T(8,128)}, u32[]{:S(2)}) copy-start(f32[32,32]{0,1:T(8,128)} %custom-call.12) | copy-start | bytes 12292
  1052.0 135.4 %copy-start.6 = (f32[32,32]{1,0:T(8,128)S(1)}, f32[32,32]{1,0:T(8,128)}, u32[]{:S(2)}) copy-start(f32[32,32]{1,0:T(8,128)} %copy-done) | copy-start | bytes 12292
  1097.8 134.2 %copy-start.17 = (f32[32,32]{0,1:T(8,128)S(1)}, f32[32,32]{0,1:T(8,128)}, u32[]{:S(2)}) copy-start(f32[32,32]{0,1:T(8,128)} %custom-call.14) | copy-start | bytes 12292
  1141.7 143.6 %copy-start.7 = (f32[32,32]{1,0:T(8,128)S(1)}, f32[32,32]{1,0:T(8,128)}, u32[]{:S(2)}) copy-start(f32[32,32]{1,0:T(8,128)} %copy-done) | copy-start | bytes 12292
  1231.3 143.4 %copy-start.8 = (f32[32,32]{1,0:T(8,128)S(1)}, f32[32,32]{1,0:T(8,128)}, u32[]{:S(2)}) copy-start(f32[32,32]{1,0:T(8,128)} %copy-done) | copy-start | bytes 12292
  1281.5 182.6 %copy-start.9 = (f32[32,32]{1,0:T(8,128)S(1)}, f32[32,32]{1,0:T(8,128)}, u32[]{:S(2)}) copy-start(f32[32,32]{1,0:T(8,128)} %copy-done) | copy-start | bytes 12292
  1329.6 223.8 %copy-start.10 = (f32[32,32]{1,0:T(8,128)S(1)}, f32[32,32]{1,0:T(8,128)}, u32[]{:S(2)}) copy-start(f32[32,32]{1,0:T(8,128)} %copy-done) | copy-start | bytes 12292
  1464.1 186.3 %copy-start.11 = (f32[32,32]{1,0:T(8,128)S(1)}, f32[32,32]{1,0:T(8,128)}, u32[]{:S(2)}) copy-start(f32[32,32]{1,0:T(8,128)} %copy-done) | copy-start | bytes 12292
  1508.4 231.2 %copy-start.12 = (f32[32,32]{1,0:T(8,128)S(1)}, f32[32,32]{1,0:T(8,128)}, u32[]{:S(2)}) copy-start(f32[32,32]{1,0:T(8,128)} %copy-done) | copy-start | bytes 12292
  1597.4 231.5 %copy-start.13 = (f32[32,32]{1,0:T(8,128)S(1)}, f32[32,32]{1,0:T(8,128)}, u32[]{:S(2)}) copy-start(f32[32,32]{1,0:T(8,128)} %copy-done) | copy-start | bytes 12292
  1650.4 267.6 %copy-start.14 = (f32[32,32]{1,0:T(8,128)S(1)}, f32[32,32]{1,0:T(8,128)}, u32[]{:S(2)}) copy-start(f32[32,32]{1,0:T(8,128)} %copy-done) | copy-start | bytes 12292
  1872.4 102.7 %copy-start.23 = (f32[32,32]{0,1:T(8,128)S(1)}, f32[32,32]{0,1:T(8,128)}, u32[]{:S(2)}) copy-start(f32[32,32]{0,1:T(8,128)} %custom-call.30) | copy-start | bytes 12292
  1918.0 102.1 %copy-start.1 = (f32[32,32]{1,0:T(8,128)S(1)}, f32[32,32]{1,0:T(8,128)}, u32[]{:S(2)}) copy-start(f32[32,32]{1,0:T(8,128)} %copy-done) | copy-start | bytes 12292
  2091.8 0.7 copy-start.25
Sparse Core Ops, SparseCore 0:
  66.2 272.8 all-reduce.4
  341.5 83.6 all-reduce.6
